TPU v7x, 128 devices: a whole 4x4x4 slice. The times are simulated.
128 devices in a mesh: gene: 8 (over y, x_lo), bin: 16 (over z, x_hi, core).
Axes of the slice: x: 4 (x_hi: 2, x_lo: 2; x = x_hi * 2 + x_lo), y: 4, z: 4, core: 2. Of those that a mesh axis runs over, the one named last changes fastest.
Arguments:
- counts: bfloat16 [49152, 18432], P('bin', 'gene'), may hold values from 2 to 80
- factors: float32 [49152, 256], P('bin'), may hold values from 0.01 to 1
- loadings: float32 [256, 18432], P(None, 'gene'), may hold values from 0.01 to 1
- position: int32 [49152], P('bin'), may hold values from 0 to 49151, as said below
- edge_codes: int32 [192, 256], P('bin'), may hold values from 1 to 15
Outputs:
- factors_new: float32 [49152, 256], P('bin')
- loadings_new: float32 [256, 18432], P(None, 'gene')
Inputs may be any that keep to these rules, and one draw needn't show every extreme that they name: Each grid position is named by exactly one barcode. The barcodes of one index s of bin (rows s * 3072 on) fall in 16 aligned groups of 192; group t holds positions in grid rows t * 12 to (t + 1) * 12 - 1, 192 from every such index.
All inputs are finite; a program needn't handle non-finite values.
Results may differ from a plain program's by a relative error of at most 0.0003.
Values sent between devices are 32-bit elements; how exact they have to be, the bound alone decides.
A program may use at most 128 MiB of HBM per device.

v0:
```python
import jax
import jax.numpy as jnp
from jax import lax
from jax.sharding import PartitionSpec as P

K = 256
G = 18432


def passed_along(block, axis, distance):
    devices = range(lax.axis_size(axis))
    route = [(i - distance, i) for i in devices if i - distance in devices]
    return lax.ppermute(block, axis, route)


def neighbour_sum(values, from_above, from_below):
    upper = jnp.concatenate([from_above[None], values[:-1]], 0)
    lower = jnp.concatenate([values[1:], from_below[None]], 0)
    beside = jnp.pad(values[:, 1:], ((0, 0), (0, 1), (0, 0))) + jnp.pad(
        values[:, :-1], ((0, 0), (1, 0), (0, 0))
    )
    return beside + 0.5 * (lower + upper)


def neighbour_first(values, from_above, from_below):
    upper = jnp.concatenate([from_above[:, None], values[:, :-1]], 1)
    lower = jnp.concatenate([values[:, 1:], from_below[:, None]], 1)
    beside = jnp.pad(values[:, :, 1:], ((0, 0), (0, 0), (0, 1))) + jnp.pad(
        values[:, :, :-1], ((0, 0), (0, 0), (1, 0))
    )
    return beside + 0.5 * (lower + upper)


def stencil_term(payload, col_width, position, edge_codes):
    bin_count = lax.axis_size("bin")
    row_count = position.shape[0]
    group_size = row_count // bin_count
    grid_rows, grid_cols = edge_codes.shape
    pos_float = position.astype(jnp.float32).reshape(bin_count, group_size)
    got_rows, got_pos = (
        lax.all_to_all(payload, "bin", split_axis=0, concat_axis=0, tiled=True),
        lax.all_to_all(pos_float, "bin", split_axis=0, concat_axis=0, tiled=True),
    )
    tile_slot = got_pos.reshape(row_count).astype(jnp.int32) - lax.axis_index("bin") * row_count
    cell_scale = edge_codes.astype(jnp.float32) / 8.0
    tile_rows = (
        jnp.zeros((row_count, col_width), jnp.float32)
        .at[tile_slot]
        .set(got_rows.reshape(row_count, col_width))
    )
    weighted = cell_scale[:, :, None] * tile_rows.reshape(grid_rows, grid_cols, col_width)
    rim_last, rim_first = (weighted[-1], weighted[0])
    upper_rows, upper_scale = passed_along((rim_last, cell_scale[-1]), "bin", 1)
    lower_rows, lower_scale = passed_along((rim_first, cell_scale[0]), "bin", -1)
    degree_grid = (
        cell_scale * neighbour_first(cell_scale[None], upper_scale[None], lower_scale[None])[0]
    )
    back_degree = degree_grid.reshape(row_count)[tile_slot]
    smooth_grid = cell_scale[:, :, None] * neighbour_sum(weighted, upper_rows, lower_rows)
    back_send = smooth_grid.reshape(row_count, col_width)[tile_slot].reshape(
        bin_count, group_size * col_width
    )
    smooth, degree = (
        lax.all_to_all(back_send, "bin", split_axis=0, concat_axis=0, tiled=True),
        lax.all_to_all(
            back_degree.reshape(bin_count, group_size),
            "bin",
            split_axis=0,
            concat_axis=0,
            tiled=True,
        ),
    )
    smooth = smooth.reshape(row_count, col_width)
    return (smooth, degree.reshape(row_count))


def on_device(counts, factors, loadings, position, edge_codes):
    bin_count = lax.axis_size("bin")
    gene_count = lax.axis_size("gene")
    row_count, width_all = factors.shape
    group_size = row_count // bin_count
    width = width_all // gene_count
    k_rows = width_all // bin_count
    gene_at = lax.axis_index("gene")
    bin_at = lax.axis_index("bin")
    load_bf = loadings.astype(jnp.bfloat16)
    right_dims = (((1,), (1,)), ((), ()))
    numer_part = lax.dot_general(counts, load_bf, right_dims, preferred_element_type=jnp.float32)
    gram_part = lax.dot_general(load_bf, load_bf, right_dims, preferred_element_type=jnp.float32)
    numer, load_gram = lax.psum_scatter(
        (numer_part, gram_part), "gene", scatter_dimension=1, tiled=True
    )
    own = lax.dynamic_slice_in_dim(factors, gene_at * width, width, 1)
    payload = own.reshape(bin_count, group_size * width)
    smooth, degree = stencil_term(payload, width, position, edge_codes)
    penalty = float(G * K) / 64.0
    denom = (
        jnp.dot(factors, load_gram, precision=lax.Precision.HIGHEST)
        + penalty * degree[:, None] * own
    )
    new_own = own * (numer + penalty * smooth) / denom
    factors_new = lax.all_gather(new_own, "gene", axis=1, tiled=True)
    fac_bf = factors_new.astype(jnp.bfloat16)
    left_dims = (((0,), (0,)), ((), ()))
    cross_part = lax.dot_general(fac_bf, counts, left_dims, preferred_element_type=jnp.float32)
    fgram_part = lax.dot_general(fac_bf, fac_bf, left_dims, preferred_element_type=jnp.float32)
    cross, fac_gram = lax.psum_scatter(
        (cross_part, fgram_part), "bin", scatter_dimension=0, tiled=True
    )
    own_load = lax.dynamic_slice_in_dim(loadings, bin_at * k_rows, k_rows, 0)
    new_load = own_load * cross / jnp.dot(fac_gram, loadings, precision=lax.Precision.HIGHEST)
    loadings_new = lax.all_gather(new_load, "bin", axis=0, tiled=True)
    return (factors_new, loadings_new)


def solution(mesh):
    placed = (P("bin", "gene"), P("bin", None), P(None, "gene"), P("bin"), P("bin", None))
    return jax.shard_map(
        on_device,
        mesh=mesh,
        in_specs=placed,
        out_specs=(P("bin", None), P(None, "gene")),
        check_vma=False,
    )
```

profile of v0, /device:TPU:1, one launch (start us, length us, event | category | flops | bytes accessed | tf_op | source)
XLA Modules:
  0.0 449.5 jit_solution(1883265635426053663)
XLA Ops:
  7.2 3.8 convolution_bitcast_fusion.1
  11.1 11.2 %fusion.9 = f32[3072,256]{0,1:T(8,128)} fusion(bf16[3072,2304]{1,0:T(8,128)(2,1)} %param.5, f32[256,2304]{1,0:T(8,128)} %param.7), kind=kOutput, calls=%fused_computation.15 | convolution fusion | flops 3624468480 | bytes 19660800 | tf_op jit(solution)/shard_map/dot_general | solution.py:88
  23.7 9.3 %all-to-all-start = ((f32[16,1,192]{2,1,0:T(1,128)}), f32[16,1,192]{2,1,0:T(1,128)S(1)}, u32[]{:S(2)}, u32[]{:S(2)}) async-start(f32[16,1,192]{2,1,0:T(1,128)} %all_to_all.24), calls=%async_computation.1 | async-start | bytes 32768 | tf_op jit(solution)/shard_map/all_to_all | solution.py:42
  33.6 5.0 %collective-permute-start.3 = (f32[256]{0:T(256)S(1)}, f32[256]{0:T(256)S(1)}, u32[]{:S(2)}, u32[]{:S(2)}) collective-permute-start(f32[256]{0:T(256)S(1)} %bitcast.48), channel_id=1, source_target_pairs={{0,1},{1,2},{2,3},{3,4},{4,5},{5,6},{6,7},{7,8},{8,9},{9,10},{10,1... | collective-permute-start | bytes 3080 | tf_op jit(solution)/shard_map/ppermute | solution.py:13
  38.6 1.9 collective-permute-start.2
  42.2 2.8 all_to_all.32
  46.1 7.0 %all-to-all-start.1 = ((f32[16,1,6144]{2,1,0:T(1,128)}), f32[16,1,6144]{2,1,0:T(1,128)S(1)}, u32[]{:S(2)}, u32[]{:S(2)}) async-start(f32[16,1,6144]{2,1,0:T(1,128)} %all_to_all.32), calls=%async_computation.2 | async-start | bytes 786432 | tf_op jit(solution)/shard_map/all_to_all | solution.py:41
  57.8 30.6 %gather_fusion.1 = f32[3072]{0:T(1024)} fusion(f32[3072]{0:T(1024)S(1)} %reshape.142, s32[3072]{0:T(1024)} %broadcast_clamp_fusion), kind=kCustom, calls=%fused_computation.1 | custom fusion | bytes 36864 | tf_op jit(solution)/shard_map/gather | solution.py:58
  89.8 7.2 %all-to-all-start.3 = ((f32[16,1,192]{2,1,0:T(1,128)}), f32[16,1,192]{2,1,0:T(1,128)}, u32[]{:S(2)}, u32[]{:S(2)}) async-start(f32[16,1,192]{2,1,0:T(1,128)} %all_to_all.30), calls=%async_computation.4 | async-start | bytes 32768 | tf_op jit(solution)/shard_map/all_to_all | solution.py:65
  98.9 2.7 reshape.163
  101.6 9.6 %scatter_custom_fusion = f32[3072,32]{1,0:T(8,128)} fusion(s32[3072]{0:T(1024)} %bitcast.42, f32[3072,32]{1,0:T(8,128)} %reshape.163, f32[]{:T(128)} %constant.7.clone.1), kind=kCustom, calls=%fused_computation.12 | custom fusion | bytes 393728 | tf_op jit(solution)/shard_map/scatter | solution.py:49
  111.2 2.9 copy.58
  115.2 2.1 collective-permute-start
  117.3 5.2 %collective-permute-start.1 = (f32[256,32]{0,1:T(8,128)S(1)}, f32[256,32]{0,1:T(8,128)S(1)}, u32[]{:S(2)}, u32[]{:S(2)}) collective-permute-start(f32[256,32]{0,1:T(8,128)S(1)} %bitcast.44), channel_id=1, source_target_pairs={{0,1},{1,2},{2,3},{3,4},{4,5},{5,6},{6,7},{7,8},{8,9},{9,10},{10,1... | collective-permute-start | bytes 98312 | tf_op jit(solution)/shard_map/ppermute | solution.py:13
  124.5 2.7 copy.52
  127.2 12.2 %gather_fusion = f32[3072,32]{1,0:T(8,128)} fusion(f32[3072,32]{1,0:T(8,128)} %bitcast.39, s32[3072]{0:T(1024)S(1)} %copy-done.4), kind=kCustom, calls=%fused_computation | custom fusion | bytes 798720 | tf_op jit(solution)/shard_map/gather | solution.py:60
  139.4 2.8 all_to_all.33
  142.3 9.0 %all-to-all-start.2 = ((f32[16,1,6144]{2,1,0:T(1,128)}), f32[16,1,6144]{2,1,0:T(1,128)S(1)}, u32[]{:S(2)}, u32[]{:S(2)}) async-start(f32[16,1,6144]{2,1,0:T(1,128)} %all_to_all.33), calls=%async_computation.3 | async-start | bytes 786432 | tf_op jit(solution)/shard_map/all_to_all | solution.py:64
  151.3 2.6 copy.61
  155.4 5.8 %all-to-all-done.2 = f32[16,1,6144]{2,1,0:T(1,128)S(1)} async-done(((f32[16,1,6144]{2,1,0:T(1,128)}), f32[16,1,6144]{2,1,0:T(1,128)S(1)}, u32[]{:S(2)}, u32[]{:S(2)}) %all-to-all-start.2) | async-done | bytes 393248 | tf_op jit(solution)/shard_map/all_to_all | solution.py:64
  163.0 2.7 mul.92
  165.7 2.6 copy.54
  168.3 4.8 %fusion.1 = f32[3072,32]{0,1:T(8,128)} fusion(f32[3072,256]{1,0:T(8,128)S(1)} %copy-done, f32[3072,32]{0,1:T(8,128)S(1)} %copy-done.1, f32[3072,32]{0,1:T(8,128)} %reduce-scatter.7.cloned.1.call-done, f32[3072,32]{0,1:T(8,128)} %copy.54, f32[3072]{0:T(1024)S(1)} %copy-done.8, f32[32,256]{1,0:T(8,128)} %reduce-scatter.13.cloned.1.call-done), kind=kOutput, calls=%fused_computation.5 | convolution fusion | flops 302481408 | bytes 4763648 | tf_op jit(solution)/shard_map/dot_general | solution.py:98
  173.2 68.6 %all-gather.3.cloned.1.call-done = f32[3072,256]{0,1:T(8,128)} async-done(((f32[3072,32]{0,1:T(8,128)}), f32[3072,256]{0,1:T(8,128)}) %all-gather.3.cloned.1.call-update) | async-done | bytes 3145744 | tf_op jit(solution)/shard_map/all_gather | solution.py:102
  241.8 4.2 fusion.2
  246.1 11.2 %fusion.4 = f32[256,2304]{1,0:T(8,128)} fusion(bf16[3072,2304]{1,0:T(8,128)(2,1)} %param.5, f32[3072,256]{0,1:T(8,128)} %all-gather.3.cloned.1.call-done), kind=kOutput, calls=%fused_computation.10 | convolution fusion | flops 3624665088 | bytes 19660800 | tf_op jit(solution)/shard_map/dot_general | solution.py:105
  257.3 52.2 %reduce-scatter.11.cloned.1.call-done = f32[16,256]{1,0:T(8,128)} async-done(((f32[256,256]{1,0:T(8,128)}), f32[16,256]{1,0:T(8,128)}) %reduce-scatter.11.cloned.1.call-update) | async-done | bytes 16400 | tf_op jit(solution)/shard_map/reduce_scatter | solution.py:107
  309.6 76.3 %reduce-scatter.9.cloned.1.call-done = f32[16,2304]{1,0:T(8,128)} async-done(((f32[256,2304]{1,0:T(8,128)}), f32[16,2304]{1,0:T(8,128)}) %reduce-scatter.9.cloned.1.call-update) | async-done | bytes 147472 | tf_op jit(solution)/shard_map/reduce_scatter | solution.py:107
  385.9 3.5 convolution_divide_fusion
  389.5 3.5 copy.56
  393.0 46.4 %all-gather.5.cloned.1.call-done = f32[256,2304]{1,0:T(8,128)} async-done(((f32[16,2304]{1,0:T(8,128)}), f32[256,2304]{1,0:T(8,128)}) %all-gather.5.cloned.1.call-update) | async-done | bytes 2359312 | tf_op jit(solution)/shard_map/all_gather | solution.py:112
  439.4 3.2 copy.69
  (68 shorter events, 19.2 us)
Async XLA Ops:
  7.2 33.5 %copy-start = (f32[3072,256]{1,0:T(8,128)S(1)}, f32[3072,256]{1,0:T(8,128)}, u32[]{:S(2)}) copy-start(f32[3072,256]{1,0:T(8,128)} %param.6) | copy-start | bytes 9437188
  7.2 161.1 %reduce-scatter.13.cloned.1.call-start = ((), (), s32[]{:S(2)}) async-start(), calls=%async_computation.13 | async-start | bytes 294912
  11.0 157.3 %reduce-scatter.7.cloned.1.call-start = ((), (), s32[]{:S(2)}) async-start(), calls=%async_computation.8 | async-start | bytes 3538944 | tf_op jit(solution)/shard_map/reduce_scatter | solution.py:90
  22.3 0.7 copy-start.9
  22.3 10.7 %copy-start.5 = (s32[12,256]{1,0:T(8,128)S(1)}, s32[12,256]{1,0:T(8,128)}, u32[]{:S(2)}) copy-start(s32[12,256]{1,0:T(8,128)} %param.9) | copy-start | bytes 36868
  23.7 21.8 %all-to-all-start = ((f32[16,1,192]{2,1,0:T(1,128)}), f32[16,1,192]{2,1,0:T(1,128)S(1)}, u32[]{:S(2)}, u32[]{:S(2)}) async-start(f32[16,1,192]{2,1,0:T(1,128)} %all_to_all.24), calls=%async_computation.1 | async-start | bytes 32768 | tf_op jit(solution)/shard_map/all_to_all | solution.py:42
  33.0 0.6 copy-start.2
  33.6 11.5 %collective-permute-start.3 = (f32[256]{0:T(256)S(1)}, f32[256]{0:T(256)S(1)}, u32[]{:S(2)}, u32[]{:S(2)}) collective-permute-start(f32[256]{0:T(256)S(1)} %bitcast.48), channel_id=1, source_target_pairs={{0,1},{1,2},{2,3},{3,4},{4,5},{5,6},{6,7},{7,8},{8,9},{9,10},{10,1... | collective-permute-start | bytes 3080 | tf_op jit(solution)/shard_map/ppermute | solution.py:13
  38.6 6.8 %collective-permute-start.2 = (f32[256]{0:T(256)S(1)}, f32[256]{0:T(256)S(1)}, u32[]{:S(2)}, u32[]{:S(2)}) collective-permute-start(f32[256]{0:T(256)S(1)} %bitcast.47), channel_id=1, source_target_pairs={{1,0},{2,1},{3,2},{4,3},{5,4},{6,5},{7,6},{8,7},{9,8},{10,9},{11,1... | collective-permute-start | bytes 3080 | tf_op jit(solution)/shard_map/ppermute | solution.py:13
  45.5 0.6 copy-start.6
  46.1 43.8 %all-to-all-start.1 = ((f32[16,1,6144]{2,1,0:T(1,128)}), f32[16,1,6144]{2,1,0:T(1,128)S(1)}, u32[]{:S(2)}, u32[]{:S(2)}) async-start(f32[16,1,6144]{2,1,0:T(1,128)} %all_to_all.32), calls=%async_computation.2 | async-start | bytes 786432 | tf_op jit(solution)/shard_map/all_to_all | solution.py:41
  56.6 0.6 copy-start.7
  89.8 52.4 %all-to-all-start.3 = ((f32[16,1,192]{2,1,0:T(1,128)}), f32[16,1,192]{2,1,0:T(1,128)}, u32[]{:S(2)}, u32[]{:S(2)}) async-start(f32[16,1,192]{2,1,0:T(1,128)} %all_to_all.30), calls=%async_computation.4 | async-start | bytes 32768 | tf_op jit(solution)/shard_map/all_to_all | solution.py:65
  98.9 15.2 %copy-start.3 = (f32[12,256]{1,0:T(8,128)S(1)}, f32[12,256]{1,0:T(8,128)}, u32[]{:S(2)}) copy-start(f32[12,256]{1,0:T(8,128)} %copy-done.2) | copy-start | bytes 36868
  115.2 7.6 %collective-permute-start = (f32[256,32]{0,1:T(8,128)S(1)}, f32[256,32]{0,1:T(8,128)S(1)}, u32[]{:S(2)}, u32[]{:S(2)}) collective-permute-start(f32[256,32]{0,1:T(8,128)S(1)} %bitcast.43), channel_id=1, source_target_pairs={{1,0},{2,1},{3,2},{4,3},{5,4},{6,5},{7,6},{8,7},{9,8},{10,9},{11,1... | collective-permute-start | bytes 98312 | tf_op jit(solution)/shard_map/ppermute | solution.py:13
  117.3 6.0 %collective-permute-start.1 = (f32[256,32]{0,1:T(8,128)S(1)}, f32[256,32]{0,1:T(8,128)S(1)}, u32[]{:S(2)}, u32[]{:S(2)}) collective-permute-start(f32[256,32]{0,1:T(8,128)S(1)} %bitcast.44), channel_id=1, source_target_pairs={{0,1},{1,2},{2,3},{3,4},{4,5},{5,6},{6,7},{7,8},{8,9},{9,10},{10,1... | collective-permute-start | bytes 98312 | tf_op jit(solution)/shard_map/ppermute | solution.py:13
  123.3 3.8 copy-start.4
  142.3 18.9 %all-to-all-start.2 = ((f32[16,1,6144]{2,1,0:T(1,128)}), f32[16,1,6144]{2,1,0:T(1,128)S(1)}, u32[]{:S(2)}, u32[]{:S(2)}) async-start(f32[16,1,6144]{2,1,0:T(1,128)} %all_to_all.33), calls=%async_computation.3 | async-start | bytes 786432 | tf_op jit(solution)/shard_map/all_to_all | solution.py:64
  151.3 90.5 %all-gather.3.cloned.1.call-start = ((), (), s32[]{:S(2)}) async-start(), calls=%async_computation.9 | async-start | bytes 3538944 | tf_op jit(solution)/shard_map/all_gather | solution.py:102
  155.4 12.9 %copy-start.8 = (f32[3072]{0:T(1024)S(1)}, f32[3072]{0:T(1024)}, u32[]{:S(2)}) copy-start(f32[3072]{0:T(1024)} %mul.99) | copy-start | bytes 36868
  163.0 5.3 %copy-start.1 = (f32[3072,32]{0,1:T(8,128)S(1)}, f32[3072,32]{0,1:T(8,128)}, u32[]{:S(2)}) copy-start(f32[3072,32]{0,1:T(8,128)} %copy.61) | copy-start | bytes 1179652
  173.2 136.4 %reduce-scatter.11.cloned.1.call-start = ((), (), s32[]{:S(2)}) async-start(), calls=%async_computation.11 | async-start | bytes 278528 | tf_op jit(solution)/shard_map/reduce_scatter | solution.py:107
  246.0 139.9 %reduce-scatter.9.cloned.1.call-start = ((), (), s32[]{:S(2)}) async-start(), calls=%async_computation.10 | async-start | bytes 2506752 | tf_op jit(solution)/shard_map/reduce_scatter | solution.py:107
  257.3 182.1 %all-gather.5.cloned.1.call-start = ((), (), s32[]{:S(2)}) async-start(), calls=%async_computation.12 | async-start | bytes 2506752 | tf_op jit(solution)/shard_map/all_gather | solution.py:112
Sparse Core Ops, SparseCore 0:
  11.1 35.2 reduce-scatter.12
  49.5 75.7 reduce-scatter.6
  173.3 68.5 all-gather.2
  246.4 63.1 reduce-scatter.10
  314.5 71.3 reduce-scatter.8
  389.6 49.7 all-gather.4
where the time goes:
time: 451 us; the launch traced here: 449 us
  waiting for transfers between devices  250 us (55%)
  local copies, waits for them, and re-layouts  89.9 us (20%)
  starting transfers between devices  47 us (10%)
  matrix products  38.7 us (9%)
  between operations  14.3 us (3%)
  other arithmetic  9.34 us (2%)
    reduce_scatter x2, waiting for transfers between devices, on_device(): lax.psum_scatter((cross_part, fgram_part), 'bin', scatter_dimension=0, ti...  129 us
    all_gather x1, waiting for transfers between devices, on_device(): factors_new = lax.all_gather(new_own, 'gene', axis=1, tiled=True)  68.6 us
    all_gather x1, waiting for transfers between devices, on_device(): loadings_new = lax.all_gather(new_load, 'bin', axis=0, tiled=True)  46.4 us
    gather x1, local copies, waits for them, and re-layouts, stencil_term(): back_degree = degree_grid.reshape(row_count)[tile_slot]  30.6 us
    ppermute x4, starting transfers between devices, passed_along(): return lax.ppermute(block, axis, route)  14.2 us
    gather x1, local copies, waits for them, and re-layouts, stencil_term(): smooth_grid.reshape(row_count, col_width)[tile_slot]  12.2 us
    unnamed x25, local copies, waits for them, and re-layouts  11.9 us
    dot_general x1, matrix products, on_device(): lax.dot_general(counts, load_bf, right_dims, preferred_element_type=jnp.f...  11.2 us
  transfers between devices with their start and end apart: 14, of which 7 were waited for; matrix products, arithmetic and copies ran while one was open for 24% of the time, Pallas kernels for 0%

commit v1 on v0

--- a/solution.py
+++ b/solution.py
@@ -99,7 +99,9 @@
         + penalty * degree[:, None] * own
     )
     new_own = own * (numer + penalty * smooth) / denom
-    factors_new = lax.all_gather(new_own, "gene", axis=1, tiled=True)
+    factors_new = jnp.concatenate(
+        lax.all_to_all(jnp.stack([new_own] * lax.axis_size("gene")), "gene", 0, 0), axis=1
+    )
     fac_bf = factors_new.astype(jnp.bfloat16)
     left_dims = (((0,), (0,)), ((), ()))
     cross_part = lax.dot_general(fac_bf, counts, left_dims, preferred_element_type=jnp.float32)

time: 451 us -> 419 us (0.929)
  waiting for transfers between devices: 250 us -> 180 us
  blocking collectives: 0 us -> 40.8 us
    all_gather x1 -> x0, waiting for transfers between devices: 68.6 us -> none  [on_device(): factors_new = lax.all_gather(new_own, 'gene', axis=1, tiled=True)]
    all_to_all x0 -> x1, blocking collectives: none -> 40.8 us  [on_device(): lax.all_to_all(jnp.stack([new_own] * lax.axis_size('gene')), 'gene', 0, 0)]
    unnamed x25 -> x27, local copies, waits for them, and re-layouts: 11.9 us -> 13.3 us
  transfers between devices with their start and end apart: 14 -> 13, of which waited for: 7 -> 6; matrix products, arithmetic and copies ran while one was open for 24% -> 26% of each run, Pallas kernels for 0% -> 0%
where the time goes in v1:
time: 419 us; the launch traced here: 418 us
  waiting for transfers between devices  180 us (43%)
  local copies, waits for them, and re-layouts  91.6 us (22%)
  starting transfers between devices  47 us (11%)
  blocking collectives  40.8 us (10%)
  matrix products  35.1 us (8%)
  between operations  14 us (3%)
  other arithmetic  9.53 us (2%)
    reduce_scatter x2, waiting for transfers between devices, on_device(): lax.psum_scatter((cross_part, fgram_part), 'bin', scatter_dimension=0, ti...  127 us
    all_gather x1, waiting for transfers between devices, on_device(): loadings_new = lax.all_gather(new_load, 'bin', axis=0, tiled=True)  46.3 us
    all_to_all x1, blocking collectives, on_device(): lax.all_to_all(jnp.stack([new_own] * lax.axis_size('gene')), 'gene', 0, 0)  40.8 us
    gather x1, local copies, waits for them, and re-layouts, stencil_term(): back_degree = degree_grid.reshape(row_count)[tile_slot]  30.6 us
    ppermute x4, starting transfers between devices, passed_along(): return lax.ppermute(block, axis, route)  14.2 us
    unnamed x27, local copies, waits for them, and re-layouts  13.3 us
    gather x1, local copies, waits for them, and re-layouts, stencil_term(): smooth_grid.reshape(row_count, col_width)[tile_slot]  12.2 us
    dot_general x1, matrix products, on_device(): lax.dot_general(counts, load_bf, right_dims, preferred_element_type=jnp.f...  11.2 us
  transfers between devices with their start and end apart: 13, of which 6 were waited for; matrix products, arithmetic and copies ran while one was open for 26% of the time, Pallas kernels for 0%

profile of v1, /device:TPU:1, one launch (start us, length us, event | category | flops | bytes accessed | tf_op | source)
XLA Modules:
  0.0 417.6 jit_solution(15839921930249427284)
XLA Ops:
  7.2 3.7 convolution_bitcast_fusion.1
  11.0 11.2 %fusion.7 = f32[3072,256]{0,1:T(8,128)} fusion(bf16[3072,2304]{1,0:T(8,128)(2,1)} %param.5, f32[256,2304]{1,0:T(8,128)} %param.7), kind=kOutput, calls=%fused_computation.14 | convolution fusion | flops 3624468480 | bytes 19660800 | tf_op jit(solution)/shard_map/dot_general | solution.py:88
  23.6 9.3 %all-to-all-start = ((f32[16,1,192]{2,1,0:T(1,128)}), f32[16,1,192]{2,1,0:T(1,128)S(1)}, u32[]{:S(2)}, u32[]{:S(2)}) async-start(f32[16,1,192]{2,1,0:T(1,128)} %all_to_all.27), calls=%async_computation.1 | async-start | bytes 32768 | tf_op jit(solution)/shard_map/all_to_all | solution.py:42
  33.6 5.0 %collective-permute-start.3 = (f32[256]{0:T(256)S(1)}, f32[256]{0:T(256)S(1)}, u32[]{:S(2)}, u32[]{:S(2)}) collective-permute-start(f32[256]{0:T(256)S(1)} %bitcast.58), channel_id=1, source_target_pairs={{0,1},{1,2},{2,3},{3,4},{4,5},{5,6},{6,7},{7,8},{8,9},{9,10},{10,1... | collective-permute-start | bytes 3080 | tf_op jit(solution)/shard_map/ppermute | solution.py:13
  38.6 1.9 collective-permute-start.2
  42.2 2.8 all_to_all.36
  46.1 7.0 %all-to-all-start.1 = ((f32[16,1,6144]{2,1,0:T(1,128)}), f32[16,1,6144]{2,1,0:T(1,128)S(1)}, u32[]{:S(2)}, u32[]{:S(2)}) async-start(f32[16,1,6144]{2,1,0:T(1,128)} %all_to_all.36), calls=%async_computation.2 | async-start | bytes 786432 | tf_op jit(solution)/shard_map/all_to_all | solution.py:41
  57.8 30.6 %gather_fusion.1 = f32[3072]{0:T(1024)} fusion(f32[3072]{0:T(1024)S(1)} %reshape.152, s32[3072]{0:T(1024)} %broadcast_clamp_fusion), kind=kCustom, calls=%fused_computation.1 | custom fusion | bytes 36864 | tf_op jit(solution)/shard_map/gather | solution.py:58
  89.8 7.2 %all-to-all-start.3 = ((f32[16,1,192]{2,1,0:T(1,128)}), f32[16,1,192]{2,1,0:T(1,128)}, u32[]{:S(2)}, u32[]{:S(2)}) async-start(f32[16,1,192]{2,1,0:T(1,128)} %all_to_all.33), calls=%async_computation.4 | async-start | bytes 32768 | tf_op jit(solution)/shard_map/all_to_all | solution.py:65
  98.8 2.7 reshape.175
  101.5 9.6 %scatter_custom_fusion = f32[3072,32]{1,0:T(8,128)} fusion(s32[3072]{0:T(1024)} %bitcast.52, f32[3072,32]{1,0:T(8,128)} %reshape.175, f32[]{:T(128)} %constant.7.clone.1), kind=kCustom, calls=%fused_computation.11 | custom fusion | bytes 393728 | tf_op jit(solution)/shard_map/scatter | solution.py:49
  111.1 2.9 copy.58
  115.2 2.1 collective-permute-start
  117.2 5.2 %collective-permute-start.1 = (f32[256,32]{0,1:T(8,128)S(1)}, f32[256,32]{0,1:T(8,128)S(1)}, u32[]{:S(2)}, u32[]{:S(2)}) collective-permute-start(f32[256,32]{0,1:T(8,128)S(1)} %bitcast.54), channel_id=1, source_target_pairs={{0,1},{1,2},{2,3},{3,4},{4,5},{5,6},{6,7},{7,8},{8,9},{9,10},{10,1... | collective-permute-start | bytes 98312 | tf_op jit(solution)/shard_map/ppermute | solution.py:13
  124.4 2.7 copy.52
  127.2 12.2 %gather_fusion = f32[3072,32]{1,0:T(8,128)} fusion(f32[3072,32]{1,0:T(8,128)} %bitcast.46, s32[3072]{0:T(1024)S(1)} %copy-done.5), kind=kCustom, calls=%fused_computation | custom fusion | bytes 798720 | tf_op jit(solution)/shard_map/gather | solution.py:60
  139.4 2.8 all_to_all.37
  142.2 9.0 %all-to-all-start.2 = ((f32[16,1,6144]{2,1,0:T(1,128)}), f32[16,1,6144]{2,1,0:T(1,128)S(1)}, u32[]{:S(2)}, u32[]{:S(2)}) async-start(f32[16,1,6144]{2,1,0:T(1,128)} %all_to_all.37), calls=%async_computation.3 | async-start | bytes 786432 | tf_op jit(solution)/shard_map/all_to_all | solution.py:64
  151.3 2.6 copy.61
  155.3 5.8 %all-to-all-done.2 = f32[16,1,6144]{2,1,0:T(1,128)S(1)} async-done(((f32[16,1,6144]{2,1,0:T(1,128)}), f32[16,1,6144]{2,1,0:T(1,128)S(1)}, u32[]{:S(2)}, u32[]{:S(2)}) %all-to-all-start.2) | async-done | bytes 393248 | tf_op jit(solution)/shard_map/all_to_all | solution.py:64
  161.1 1.8 multiply_reduce_fusion
  162.9 2.7 mul.92
  165.7 2.6 copy.54
  168.3 4.1 fusion.1
  172.7 40.8 %all_to_all.43 = f32[8,3072,32]{1,2,0:T(8,128)S(1)} all-to-all(f32[8,3072,32]{1,2,0:T(8,128)S(1)} %stack.2), channel_id=1, replica_groups=mesh['gene'=8,'bin'=16] {'gene'}, dimensions={0} | all-to-all | bytes 6291456 | tf_op jit(solution)/shard_map/all_to_all | solution.py:103
  216.5 11.2 %fusion.2 = f32[256,2304]{1,0:T(8,128)} fusion(bf16[3072,2304]{1,0:T(8,128)(2,1)} %param.5, f32[3072,256]{0,1:T(8,128)} %bitcast.47), kind=kOutput, calls=%fused_computation.8 | convolution fusion | flops 3624665088 | bytes 19660800 | tf_op jit(solution)/shard_map/dot_general | solution.py:107
  227.8 50.3 %reduce-scatter.11.cloned.1.call-done = f32[16,256]{1,0:T(8,128)} async-done(((f32[256,256]{1,0:T(8,128)}), f32[16,256]{1,0:T(8,128)}) %reduce-scatter.11.cloned.1.call-update) | async-done | bytes 16400 | tf_op jit(solution)/shard_map/reduce_scatter | solution.py:109
  278.0 76.4 %reduce-scatter.9.cloned.1.call-done = f32[16,2304]{1,0:T(8,128)} async-done(((f32[256,2304]{1,0:T(8,128)}), f32[16,2304]{1,0:T(8,128)}) %reduce-scatter.9.cloned.1.call-update) | async-done | bytes 147472 | tf_op jit(solution)/shard_map/reduce_scatter | solution.py:109
  354.4 3.5 convolution_divide_fusion
  358.0 3.5 copy.56
  361.5 46.3 %all-gather.2.cloned.1.call-done = f32[256,2304]{1,0:T(8,128)} async-done(((f32[16,2304]{1,0:T(8,128)}), f32[256,2304]{1,0:T(8,128)}) %all-gather.2.cloned.1.call-update) | async-done | bytes 2359312 | tf_op jit(solution)/shard_map/all_gather | solution.py:114
  407.8 3.2 copy.69
  (70 shorter events, 20.6 us)
Async XLA Ops:
  7.2 33.5 %copy-start = (f32[3072,256]{1,0:T(8,128)S(1)}, f32[3072,256]{1,0:T(8,128)}, u32[]{:S(2)}) copy-start(f32[3072,256]{1,0:T(8,128)} %param.6) | copy-start | bytes 9437188
  7.2 161.1 %reduce-scatter.13.cloned.1.call-start = ((), (), s32[]{:S(2)}) async-start(), calls=%async_computation.13 | async-start | bytes 294912
  11.0 157.3 %reduce-scatter.7.cloned.1.call-start = ((), (), s32[]{:S(2)}) async-start(), calls=%async_computation.9 | async-start | bytes 3538944 | tf_op jit(solution)/shard_map/reduce_scatter | solution.py:90
  22.2 0.7 copy-start.10
  22.3 10.7 %copy-start.6 = (s32[12,256]{1,0:T(8,128)S(1)}, s32[12,256]{1,0:T(8,128)}, u32[]{:S(2)}) copy-start(s32[12,256]{1,0:T(8,128)} %param.9) | copy-start | bytes 36868
  23.6 21.8 %all-to-all-start = ((f32[16,1,192]{2,1,0:T(1,128)}), f32[16,1,192]{2,1,0:T(1,128)S(1)}, u32[]{:S(2)}, u32[]{:S(2)}) async-start(f32[16,1,192]{2,1,0:T(1,128)} %all_to_all.27), calls=%async_computation.1 | async-start | bytes 32768 | tf_op jit(solution)/shard_map/all_to_all | solution.py:42
  33.0 0.6 copy-start.3
  33.6 11.5 %collective-permute-start.3 = (f32[256]{0:T(256)S(1)}, f32[256]{0:T(256)S(1)}, u32[]{:S(2)}, u32[]{:S(2)}) collective-permute-start(f32[256]{0:T(256)S(1)} %bitcast.58), channel_id=1, source_target_pairs={{0,1},{1,2},{2,3},{3,4},{4,5},{5,6},{6,7},{7,8},{8,9},{9,10},{10,1... | collective-permute-start | bytes 3080 | tf_op jit(solution)/shard_map/ppermute | solution.py:13
  38.6 6.8 %collective-permute-start.2 = (f32[256]{0:T(256)S(1)}, f32[256]{0:T(256)S(1)}, u32[]{:S(2)}, u32[]{:S(2)}) collective-permute-start(f32[256]{0:T(256)S(1)} %bitcast.57), channel_id=1, source_target_pairs={{1,0},{2,1},{3,2},{4,3},{5,4},{6,5},{7,6},{8,7},{9,8},{10,9},{11,1... | collective-permute-start | bytes 3080 | tf_op jit(solution)/shard_map/ppermute | solution.py:13
  45.5 0.6 copy-start.7
  46.1 43.8 %all-to-all-start.1 = ((f32[16,1,6144]{2,1,0:T(1,128)}), f32[16,1,6144]{2,1,0:T(1,128)S(1)}, u32[]{:S(2)}, u32[]{:S(2)}) async-start(f32[16,1,6144]{2,1,0:T(1,128)} %all_to_all.36), calls=%async_computation.2 | async-start | bytes 786432 | tf_op jit(solution)/shard_map/all_to_all | solution.py:41
  56.6 0.6 copy-start.8
  89.8 52.4 %all-to-all-start.3 = ((f32[16,1,192]{2,1,0:T(1,128)}), f32[16,1,192]{2,1,0:T(1,128)}, u32[]{:S(2)}, u32[]{:S(2)}) async-start(f32[16,1,192]{2,1,0:T(1,128)} %all_to_all.33), calls=%async_computation.4 | async-start | bytes 32768 | tf_op jit(solution)/shard_map/all_to_all | solution.py:65
  101.5 12.5 %copy-start.4 = (f32[12,256]{1,0:T(8,128)S(1)}, f32[12,256]{1,0:T(8,128)}, u32[]{:S(2)}) copy-start(f32[12,256]{1,0:T(8,128)} %copy-done.3) | copy-start | bytes 36868
  115.2 7.6 %collective-permute-start = (f32[256,32]{0,1:T(8,128)S(1)}, f32[256,32]{0,1:T(8,128)S(1)}, u32[]{:S(2)}, u32[]{:S(2)}) collective-permute-start(f32[256,32]{0,1:T(8,128)S(1)} %bitcast.53), channel_id=1, source_target_pairs={{1,0},{2,1},{3,2},{4,3},{5,4},{6,5},{7,6},{8,7},{9,8},{10,9},{11,1... | collective-permute-start | bytes 98312 | tf_op jit(solution)/shard_map/ppermute | solution.py:13
  117.2 6.0 %collective-permute-start.1 = (f32[256,32]{0,1:T(8,128)S(1)}, f32[256,32]{0,1:T(8,128)S(1)}, u32[]{:S(2)}, u32[]{:S(2)}) collective-permute-start(f32[256,32]{0,1:T(8,128)S(1)} %bitcast.54), channel_id=1, source_target_pairs={{0,1},{1,2},{2,3},{3,4},{4,5},{5,6},{6,7},{7,8},{8,9},{9,10},{10,1... | collective-permute-start | bytes 98312 | tf_op jit(solution)/shard_map/ppermute | solution.py:13
  124.4 2.7 copy-start.5
  142.2 18.9 %all-to-all-start.2 = ((f32[16,1,6144]{2,1,0:T(1,128)}), f32[16,1,6144]{2,1,0:T(1,128)S(1)}, u32[]{:S(2)}, u32[]{:S(2)}) async-start(f32[16,1,6144]{2,1,0:T(1,128)} %all_to_all.37), calls=%async_computation.3 | async-start | bytes 786432 | tf_op jit(solution)/shard_map/all_to_all | solution.py:64
  151.2 126.8 %reduce-scatter.11.cloned.1.call-start = ((), (), s32[]{:S(2)}) async-start(), calls=%async_computation.11 | async-start | bytes 278528 | tf_op jit(solution)/shard_map/reduce_scatter | solution.py:109
  162.9 5.3 %copy-start.2 = (f32[3072,32]{0,1:T(8,128)S(1)}, f32[3072,32]{0,1:T(8,128)}, u32[]{:S(2)}) copy-start(f32[3072,32]{0,1:T(8,128)} %copy.61) | copy-start | bytes 1179652
  162.9 5.3 %copy-start.9 = (f32[3072]{0:T(1024)S(1)}, f32[3072]{0:T(1024)}, u32[]{:S(2)}) copy-start(f32[3072]{0:T(1024)} %mul.99) | copy-start | bytes 36868
  213.5 1.6 copy-start.1
  216.4 137.9 %reduce-scatter.9.cloned.1.call-start = ((), (), s32[]{:S(2)}) async-start(), calls=%async_computation.10 | async-start | bytes 2506752 | tf_op jit(solution)/shard_map/reduce_scatter | solution.py:109
  227.7 180.1 %all-gather.2.cloned.1.call-start = ((), (), s32[]{:S(2)}) async-start(), calls=%async_computation.12 | async-start | bytes 2506752 | tf_op jit(solution)/shard_map/all_gather | solution.py:114
Sparse Core Ops, SparseCore 0:
  11.1 35.2 reduce-scatter.12
  49.5 75.7 reduce-scatter.6
  216.6 61.4 reduce-scatter.10
  283.0 71.3 reduce-scatter.8
  358.1 49.7 all-gather.1
